TPU v7x, 32 devices: a whole 2x2x4 slice. The times are simulated.
32 devices in a mesh: views: 8 (over y, x, core), heads: 4 (over z).
Axes of the slice: x: 2, y: 2, z: 4, core: 2. Of those that a mesh axis runs over, the one named last changes fastest.
Arguments:
- latents: bfloat16 [32, 256, 1024], P('views'), may hold values from -6 to 6
- norm_gain: float32 [1024], replicated, may hold values from 0.25 to 1.75
- w_qkv: bfloat16 [3, 1024, 1024], P(None, None, 'heads'), may hold values from -0.1875 to 0.1875
- w_out: bfloat16 [1024, 1024], P('heads'), may hold values from -0.1875 to 0.1875
- intersection: int32 [32, 2], replicated, may hold values 0 or 1
- match_block: int32 [8192, 1], P('views'), may hold values from 0 to 7; in each aligned block of 1024 rows (0 to 1023, 1024 to 2047, ...) at most 256 rows name the same one
- match_row: int32 [8192], P('views'), may hold values from 0 to 1023
- confidence: float32 [8192], P('views'), may hold values from 0.2 to 1
Outputs:
- refined: float32 [32, 256, 1024], P('views', None, 'heads')
Inputs may be any that keep to these rules, and one draw needn't show every extreme that they name: `match_block`: among the rows of one device (1024 aligned rows), at most 256 name the same block, and some block is named by exactly 256 of them.
All inputs are finite; a program needn't handle non-finite values.
Results may differ from a plain program's by a relative error of at most 0.012.
The roundings to bfloat16 on the way count: a program that leaves them out, or rounds other values in their place, can miss the bound.
Values may be sent and summed in bfloat16 or wider, within the bound.
No kernel may reach another device: no remote copies, remote signals or barrier semaphores. Data moves between devices by JAX's collectives and lax.ppermute only.
A program may use at most 128 MiB of HBM per device.

v0:
```python
import jax
import jax.numpy as jnp
from jax import lax
from jax.sharding import PartitionSpec as P

D = 1024
HEADS = 16


neg_large = -1e30
coupling = 0.5
epsilon = 1e-06


def passed_along(x, axis, by):
    peers = lax.axis_size(axis)
    return lax.ppermute(x, axis, [(i, (i + by) % peers) for i in range(peers)])


def partial_block(queries, keys, values, head_dim):
    tokens = queries.shape[0]
    heads_here = queries.shape[1] // head_dim
    query_heads = queries.reshape(tokens, heads_here, head_dim)
    key_heads = keys.reshape(tokens, heads_here, head_dim)
    value_heads = values.reshape(tokens, heads_here, head_dim)
    scores = jnp.einsum(
        "qhd,khd->hqk", query_heads, key_heads, preferred_element_type=jnp.float32
    ) * head_dim ** (-0.5)
    maximum = jnp.max(scores, axis=-1)
    weights = jnp.exp(scores - maximum[..., None])
    totals = jnp.sum(weights, axis=-1)
    numerator = jnp.einsum(
        "hqk,khd->hqd",
        weights.astype(jnp.bfloat16),
        value_heads,
        preferred_element_type=jnp.float32,
    )
    return (maximum, totals, numerator)


def merge_into(running, piece_part, present):
    maximum, totals, numerator = running
    other_max, other_tot, other_num = piece_part
    other_max = jnp.where(present > 0, other_max, neg_large)
    highest = jnp.maximum(maximum, other_max)
    old_scale = jnp.exp(maximum - highest)
    new_scale = jnp.exp(other_max - highest) * present
    return (
        highest,
        totals * old_scale + other_tot * new_scale,
        numerator * old_scale[..., None] + other_num * new_scale[..., None],
    )


def per_device(latents, norm_gain, w_qkv, w_out, intersection, match_block, match_row, confidence):
    local_views, tokens, feature_width = latents.shape
    window = intersection.shape[1]
    sub_width = w_qkv.shape[2]
    head_dim = D // HEADS
    device_count = lax.axis_size("views")
    views_total = local_views * device_count
    first_view = lax.axis_index("views") * local_views
    head_group = lax.axis_index("heads")
    local_rows = local_views * tokens
    wide_latents = latents.astype(jnp.float32)
    mean_square = jnp.mean(wide_latents * wide_latents, axis=-1, keepdims=True)
    normed = (
        (wide_latents * lax.rsqrt(mean_square + epsilon) * norm_gain)
        .astype(jnp.bfloat16)
        .reshape(local_rows, feature_width)
    )
    joined_weight = jnp.concatenate([w_qkv[0], w_qkv[1], w_qkv[2]], axis=1)
    projected = jnp.dot(normed, joined_weight, preferred_element_type=jnp.float32).astype(
        jnp.bfloat16
    )
    projected = projected.reshape(local_views, tokens, 3 * sub_width)

    def split_parts(block):
        return (
            block[:, :sub_width],
            block[:, sub_width : 2 * sub_width],
            block[:, 2 * sub_width :],
        )

    running = []
    for source in range(local_views):
        queries, keys, values = split_parts(projected[source])
        running.append(partial_block(queries, keys, values, head_dim))
    ahead = passed_along(projected[:window], "views", -1)
    extended = jnp.concatenate([projected, ahead], axis=0)
    empty_max = jnp.full((sub_width // head_dim, tokens), neg_large, jnp.float32)
    empty_tot = jnp.zeros((sub_width // head_dim, tokens), jnp.float32)
    empty_num = jnp.zeros((sub_width // head_dim, tokens, head_dim), jnp.float32)
    outgoing = [(empty_max, empty_tot, empty_num) for slot_number in range(window)]
    for source in range(local_views):
        src_queries, src_keys, src_values = split_parts(projected[source])
        for offset in range(window):
            partner = source + offset + 1
            present = intersection[(first_view + source) % views_total, offset].astype(jnp.float32)
            par_queries, par_keys, par_values = split_parts(extended[partner])
            running[source] = merge_into(
                running[source], partial_block(src_queries, par_keys, par_values, head_dim), present
            )
            reverse_part = partial_block(par_queries, src_keys, src_values, head_dim)
            if partner < local_views:
                running[partner] = merge_into(running[partner], reverse_part, present)
            else:
                outgoing[partner - local_views] = merge_into(
                    outgoing[partner - local_views], reverse_part, present
                )
    sent_max = jnp.stack([entry[0] for entry in outgoing])
    sent_tot = jnp.stack([entry[1] for entry in outgoing])
    sent_num = jnp.stack([entry[2] for entry in outgoing])
    got_max, got_tot, got_num = passed_along((sent_max, sent_tot, sent_num), "views", 1)
    for slot_number in range(window):
        running[slot_number] = merge_into(
            running[slot_number],
            (got_max[slot_number], got_tot[slot_number], got_num[slot_number]),
            jnp.float32(1.0),
        )
    attended_views = []
    for source in range(local_views):
        maximum, totals, numerator = running[source]
        result = numerator / totals[..., None]
        attended_views.append(
            jnp.transpose(result, (1, 0, 2)).reshape(tokens, sub_width).astype(jnp.bfloat16)
        )
    attended = jnp.concatenate(attended_views, axis=0)
    group_terms = jnp.dot(attended, w_out, preferred_element_type=jnp.float32)
    summed = lax.psum_scatter(
        group_terms.astype(jnp.bfloat16), "heads", scatter_dimension=1, tiled=True
    ).astype(jnp.float32)
    own_features = lax.dynamic_slice_in_dim(
        latents.reshape(local_rows, feature_width), head_group * sub_width, sub_width, 1
    )
    layer_out = (own_features.astype(jnp.float32) + summed).astype(jnp.bfloat16)
    target_block = match_block[:, 0]
    capacity = 2 * local_rows // device_count
    onehot = (target_block[:, None] == jnp.arange(device_count, dtype=jnp.int32)[None, :]).astype(
        jnp.int32
    )
    earlier = jnp.cumsum(onehot, axis=0) - onehot
    slot_index = jnp.sum(earlier * onehot, axis=1)
    requests = (
        jnp.zeros((device_count, capacity), jnp.int32).at[target_block, slot_index].set(match_row)
    )
    row_values = layer_out[
        lax.all_to_all(requests, "views", split_axis=0, concat_axis=0, tiled=True)
    ]
    replies = lax.all_to_all(row_values, "views", split_axis=0, concat_axis=0, tiled=True)
    fetched = replies[target_block, slot_index]
    layer_wide = layer_out.astype(jnp.float32)
    refined = layer_wide + coupling * confidence[:, None] * (
        fetched.astype(jnp.float32) - layer_wide
    )
    return refined.reshape(local_views, tokens, sub_width)


def solution(mesh):
    in_specs = (
        P("views", None, None),
        P(),
        P(None, None, "heads"),
        P("heads", None),
        P(),
        P("views", None),
        P("views"),
        P("views"),
    )
    out_specs = P("views", None, "heads")
    return jax.shard_map(
        per_device, mesh=mesh, in_specs=in_specs, out_specs=out_specs, check_vma=False
    )
```

profile of v0, /device:TPU:0, one launch (start us, length us, event | category | flops | bytes accessed | tf_op | source)
XLA Modules:
  0.0 161.2 jit_solution(6106492756963043064)
XLA Ops:
  6.5 2.2 %fusion = f32[4,256]{1,0:T(4,128)S(1)} fusion(bf16[4,256,1024]{2,1,0:T(8,128)(2,1)} %param.8), kind=kLoop, calls=%fused_computation.5 | loop fusion | flops 3144704 | bytes 2101248 | tf_op jit(solution)/shard_map/reduce_sum | solution.py:66
  8.9 1.4 copy-done.1
  10.4 0.5 fusion.2
  10.9 1.8 %convolution_convert_fusion.1 = bf16[1024,768]{0,1:T(8,128)(2,1)S(1)} fusion(bf16[1024,1024]{1,0:T(8,128)(2,1)S(1)} %bitcast.549, bf16[1024,256]{1,0:T(8,128)(2,1)S(1)} %get-tuple-element.52, bf16[1024,256]{1,0:T(8,128)(2,1)S(1)} %get-tuple-element.53, bf16[1024,256]{1,0:T(8,128)(2,1)S(1)} %get-tuple-element.51), kind=kOutput, calls=%fused_computation.9 | convolution fusion | flops 1616117760 | bytes 5242880 | tf_op jit(solution)/shard_map/dot_general | solution.py:73
  12.8 1.1 copy-done.35
  14.0 1.2 copy.76
  15.1 3.4 %collective-permute-start = (bf16[2,256,768]{2,1,0:T(8,128)(2,1)}, bf16[2,256,768]{2,1,0:T(8,128)(2,1)}, u32[]{:S(2)}, u32[]{:S(2)}) collective-permute-start(bf16[2,256,768]{2,1,0:T(8,128)(2,1)} %bitcast.557), channel_id=1, source_target_pairs={{0,28},{4,0},{8,4},{12,8},{16,12},{20,16},{24,20},{28,24},{1,29},{... | collective-permute-start | bytes 2359304 | tf_op jit(solution)/shard_map/ppermute | solution.py:17
  18.5 2.3 %fusion.243 = (bf16[256,256]{0,1:T(8,128)(2,1)S(1)}, bf16[256,256]{0,1:T(8,128)(2,1)S(1)}, bf16[256,256]{0,1:T(8,128)(2,1)S(1)}, bf16[256,256]{0,1:T(8,128)(2,1)...) fusion(bf16[1024,768]{0,1:T(8,128)(2,1)} %copy-done.35), kind=kLoop, calls=%fused_computation.378 | loop fusion | bytes 3145728 | tf_op jit(solution)/shard_map/slice | solution.py:80
  24.6 0.4 fusion.261
  25.4 0.9 fusion.87
  26.2 0.9 fusion.83
  27.2 0.9 fusion.77
  28.1 0.9 fusion.73
  29.0 0.9 fusion.69
  29.9 0.9 fusion.65
  30.8 0.8 fusion.57
  31.5 0.7 constant_dynamic-slice_fusion.3
  37.2 1.3 fusion.265
  38.5 1.4 fusion.264
  40.0 1.0 fusion.53
  41.0 1.2 slice_bitcast_fusion.4
  42.1 0.9 fusion.244
  43.0 1.0 copy.46
  44.0 1.9 %fusion.248 = (f32[4,256]{1,0:T(4,128)}, f32[4,256,256]{1,2,0:T(8,128)}) fusion(bf16[256,4,64]{0,2,1:T(8,128)(2,1)S(1)} %bitcast.509, bf16[256,4,64]{0,2,1:T(8,128)(2,1)S(1)} %bitcast.553), kind=kOutput, calls=%fused_computation.383 | convolution fusion | flops 34077696 | bytes 1314816 | tf_op jit(solution)/shard_map/qhd,khd->hqk/dot_general | solution.py:26
  46.0 1.9 %fusion.252 = (f32[4,256]{1,0:T(4,128)}, f32[4,256,256]{1,2,0:T(8,128)}) fusion(bf16[256,4,64]{0,2,1:T(8,128)(2,1)S(1)} %bitcast.520, bf16[256,4,64]{0,2,1:T(8,128)(2,1)S(1)} %bitcast.554), kind=kOutput, calls=%fused_computation.387 | convolution fusion | flops 34077696 | bytes 1314816 | tf_op jit(solution)/shard_map/qhd,khd->hqk/dot_general | solution.py:26
  47.9 1.0 copy.33
  48.9 1.3 fusion.257
  50.2 1.4 fusion.258
  51.6 1.0 copy.53
  52.6 1.9 %fusion.247 = (f32[4,256]{1,0:T(4,128)}, f32[4,256,256]{1,2,0:T(8,128)}) fusion(bf16[256,4,64]{0,2,1:T(8,128)(2,1)S(1)} %bitcast.510, bf16[256,4,64]{0,2,1:T(8,128)(2,1)S(1)} %bitcast.558), kind=kOutput, calls=%fused_computation.382 | convolution fusion | flops 34077696 | bytes 1314816 | tf_op jit(solution)/shard_map/qhd,khd->hqk/dot_general | solution.py:26
  54.5 1.0 copy.47
  55.6 0.8 copy.54
  57.0 0.7 copy-done.27
  65.4 3.4 %collective-permute-done.3 = f32[2,4,256]{2,1,0:T(4,128)S(1)} collective-permute-done((f32[2,4,256]{2,1,0:T(4,128)S(1)}, f32[2,4,256]{2,1,0:T(4,128)S(1)}, u32[]{:S(2)}, u32[]{:S(2)}) %collective-permute-start.3) | collective-permute-done | bytes 8224 | tf_op jit(solution)/shard_map/ppermute | solution.py:17
  70.1 0.5 copy-done.25
  71.7 0.6 copy-done.32
  72.6 2.1 %convolution_convert_fusion = bf16[1024,1024]{1,0:T(8,128)(2,1)} fusion(bf16[256,1024]{1,0:T(8,128)(2,1)S(1)} %copy-done, bf16[256,256]{0,1:T(8,128)(2,1)S(1)} %bitcast.569, bf16[256,256]{0,1:T(8,128)(2,1)S(1)} %bitcast.568, bf16[256,256]{0,1:T(8,128)(2,1)S(1)} %bitcast.570, bf16[256,256]{0,1:T(8,128)(2,1)S(1)} %bitcast.571), kind=kOutput, calls=%fused_computation.8 | convolution fusion | flops 540016640 | bytes 3145728 | tf_op jit(solution)/shard_map/dot_general | solution.py:129
  74.7 2.3 %reduce-window.6 = s32[8,8,128]{2,1,0:T(8,128)S(1)} reduce-window(s32[8,8,128]{2,1,0:T(8,128)S(1)} %fusion.155, s32[]{:T(128)} %constant.64.clone.1), window={size=1x1x128 pad=0_0x0_0x127_0}, to_apply=%region_42.43 | reduce-window | flops 1040384 | bytes 65540 | tf_op jit(solution)/shard_map/reduce-window
  77.8 5.0 %scatter_custom_fusion = s32[2048]{0:T(1024)} fusion(s32[1024]{0:T(1024)S(1)} %broadcast_select_fusion, s32[1024]{0:T(1024)} %param.14, s32[]{:T(128)} %constant.64.clone.1), kind=kCustom, calls=%fused_computation.343 | custom fusion | bytes 8704
  82.8 3.3 %all-to-all-start = ((s32[8,1,256]{2,1,0:T(1,128)}), s32[8,1,256]{2,1,0:T(1,128)S(1)}, u32[]{:S(2)}, u32[]{:S(2)}) async-start(s32[8,1,256]{2,1,0:T(1,128)} %bitcast.88), calls=%async_computation.1 | async-start | bytes 16384 | tf_op jit(solution)/shard_map/all_to_all | solution.py:148
  86.2 4.6 %all-to-all-done = s32[8,1,256]{2,1,0:T(1,128)S(1)} async-done(((s32[8,1,256]{2,1,0:T(1,128)}), s32[8,1,256]{2,1,0:T(1,128)S(1)}, u32[]{:S(2)}, u32[]{:S(2)}) %all-to-all-start) | async-done | bytes 8224 | tf_op jit(solution)/shard_map/all_to_all | solution.py:148
  90.8 27.0 %reduce-scatter.2.cloned.1.call-done = bf16[1024,256]{1,0:T(8,128)(2,1)} async-done(((bf16[1024,1024]{1,0:T(8,128)(2,1)}), bf16[1024,256]{1,0:T(8,128)(2,1)}) %reduce-scatter.2.cloned.1.call-update) | async-done | bytes 524304 | tf_op jit(solution)/shard_map/reduce_scatter | solution.py:130
  117.9 1.2 add_convert_fusion
  119.1 9.1 %gather_fusion = bf16[2048,256]{1,0:T(8,128)(2,1)} fusion(bf16[1024,256]{1,0:T(8,128)(2,1)S(1)} %add_convert_fusion, s32[2048]{0:T(1024)S(1)} %broadcast_clamp_fusion), kind=kCustom, calls=%fused_computation | custom fusion | bytes 2105344 | tf_op jit(solution)/shard_map/gather | solution.py:147
  128.1 3.8 %all-to-all-start.1 = ((bf16[8,256,256]{2,1,0:T(8,128)(2,1)}), bf16[8,256,256]{2,1,0:T(8,128)(2,1)S(1)}, u32[]{:S(2)}, u32[]{:S(2)}) async-start(bf16[8,256,256]{2,1,0:T(8,128)(2,1)} %bitcast.91), calls=%async_computation.2 | async-start | bytes 2097152 | tf_op jit(solution)/shard_map/all_to_all | solution.py:150
  131.9 15.4 %all-to-all-done.1 = bf16[8,256,256]{2,1,0:T(8,128)(2,1)S(1)} async-done(((bf16[8,256,256]{2,1,0:T(8,128)(2,1)}), bf16[8,256,256]{2,1,0:T(8,128)(2,1)S(1)}, u32[]{:S(2)}, u32[]{:S(2)}) %all-to-all-start.1) | async-done | bytes 1048608 | tf_op jit(solution)/shard_map/all_to_all | solution.py:150
  147.3 5.8 %gather_fusion.1 = bf16[1024,256]{1,0:T(8,128)(2,1)S(1)} fusion(bf16[8,256,256]{2,1,0:T(8,128)(2,1)S(1)} %all-to-all-done.1, s32[1024]{0:T(1024)S(1)} %bitcast.499), kind=kCustom, calls=%fused_computation.1 | custom fusion | bytes 1056768 | tf_op jit(solution)/shard_map/gather | solution.py:151
  153.1 1.3 convert_add_fusion
  (250 shorter events, 15.4 us)
Async XLA Ops:
  6.5 66.0 %copy-start = (bf16[256,1024]{1,0:T(8,128)(2,1)S(1)}, bf16[256,1024]{1,0:T(8,128)(2,1)}, u32[]{:S(2)}) copy-start(bf16[256,1024]{1,0:T(8,128)(2,1)} %param.11) | copy-start | bytes 1572868
  6.5 111.3 %reduce-scatter.2.cloned.1.call-start = ((), (), s32[]{:S(2)}) async-start(), calls=%async_computation.3 | async-start | bytes 2621440 | tf_op jit(solution)/shard_map/reduce_scatter | solution.py:130
  15.1 25.8 %collective-permute-start = (bf16[2,256,768]{2,1,0:T(8,128)(2,1)}, bf16[2,256,768]{2,1,0:T(8,128)(2,1)}, u32[]{:S(2)}, u32[]{:S(2)}) collective-permute-start(bf16[2,256,768]{2,1,0:T(8,128)(2,1)} %bitcast.557), channel_id=1, source_target_pairs={{0,28},{4,0},{8,4},{12,8},{16,12},{20,16},{24,20},{28,24},{1,29},{... | collective-permute-start | bytes 2359304 | tf_op jit(solution)/shard_map/ppermute | solution.py:17
  20.8 3.8 %copy-start.38 = (bf16[256,256]{0,1:T(8,128)(2,1)}, bf16[256,256]{0,1:T(8,128)(2,1)S(1)}, u32[]{:S(2)}) copy-start(bf16[256,256]{0,1:T(8,128)(2,1)S(1)} %get-tuple-element.50) | copy-start | bytes 393220
  20.8 4.2 %copy-start.37 = (bf16[256,256]{0,1:T(8,128)(2,1)}, bf16[256,256]{0,1:T(8,128)(2,1)S(1)}, u32[]{:S(2)}) copy-start(bf16[256,256]{0,1:T(8,128)(2,1)S(1)} %get-tuple-element.39) | copy-start | bytes 393220
  21.1 5.1 %copy-start.20 = (f32[4,256,256]{1,2,0:T(8,128)}, f32[4,256,256]{1,2,0:T(8,128)S(1)}, u32[]{:S(2)}) copy-start(f32[4,256,256]{1,2,0:T(8,128)S(1)} %get-tuple-element.84) | copy-start | bytes 3145732
  21.2 5.1 %copy-start.58 = (f32[4,256]{1,0:T(4,128)}, f32[4,256]{1,0:T(4,128)S(1)}, u32[]{:S(2)}) copy-start(f32[4,256]{1,0:T(4,128)S(1)} %get-tuple-element.83) | copy-start | bytes 12292
  21.5 4.7 %copy-start.12 = (f32[4,256,256]{1,2,0:T(8,128)}, f32[4,256,256]{1,2,0:T(8,128)S(1)}, u32[]{:S(2)}) copy-start(f32[4,256,256]{1,2,0:T(8,128)S(1)} %get-tuple-element.92) | copy-start | bytes 3145732
  21.5 4.7 %copy-start.50 = (f32[4,256]{1,0:T(4,128)}, f32[4,256]{1,0:T(4,128)S(1)}, u32[]{:S(2)}) copy-start(f32[4,256]{1,0:T(4,128)S(1)} %get-tuple-element.91) | copy-start | bytes 12292
  21.9 5.2 %copy-start.10 = (f32[4,256,256]{1,2,0:T(8,128)}, f32[4,256,256]{1,2,0:T(8,128)S(1)}, u32[]{:S(2)}) copy-start(f32[4,256,256]{1,2,0:T(8,128)S(1)} %get-tuple-element.100) | copy-start | bytes 3145732
  21.9 5.2 %copy-start.48 = (f32[4,256]{1,0:T(4,128)}, f32[4,256]{1,0:T(4,128)S(1)}, u32[]{:S(2)}) copy-start(f32[4,256]{1,0:T(4,128)S(1)} %get-tuple-element.99) | copy-start | bytes 12292
  22.3 4.9 %copy-start.8 = (f32[4,256,256]{1,2,0:T(8,128)}, f32[4,256,256]{1,2,0:T(8,128)S(1)}, u32[]{:S(2)}) copy-start(f32[4,256,256]{1,2,0:T(8,128)S(1)} %get-tuple-element.98) | copy-start | bytes 3145732
  22.3 4.9 %copy-start.46 = (f32[4,256]{1,0:T(4,128)}, f32[4,256]{1,0:T(4,128)S(1)}, u32[]{:S(2)}) copy-start(f32[4,256]{1,0:T(4,128)S(1)} %get-tuple-element.97) | copy-start | bytes 12292
  23.0 5.0 %copy-start.14 = (f32[4,256,256]{1,2,0:T(8,128)}, f32[4,256,256]{1,2,0:T(8,128)S(1)}, u32[]{:S(2)}) copy-start(f32[4,256,256]{1,2,0:T(8,128)S(1)} %get-tuple-element.102) | copy-start | bytes 3145732
  23.0 5.0 %copy-start.52 = (f32[4,256]{1,0:T(4,128)}, f32[4,256]{1,0:T(4,128)S(1)}, u32[]{:S(2)}) copy-start(f32[4,256]{1,0:T(4,128)S(1)} %get-tuple-element.101) | copy-start | bytes 12292
  23.4 5.6 %copy-start.2 = (f32[4,256,256]{1,2,0:T(8,128)}, f32[4,256,256]{1,2,0:T(8,128)S(1)}, u32[]{:S(2)}) copy-start(f32[4,256,256]{1,2,0:T(8,128)S(1)} %get-tuple-element.112) | copy-start | bytes 3145732
  23.8 5.2 %copy-start.29 = (f32[4,256,256]{1,2,0:T(8,128)}, f32[4,256,256]{1,2,0:T(8,128)S(1)}, u32[]{:S(2)}) copy-start(f32[4,256,256]{1,2,0:T(8,128)S(1)} %get-tuple-element.110) | copy-start | bytes 3145732
  23.8 5.2 %copy-start.65 = (f32[4,256]{1,0:T(4,128)}, f32[4,256]{1,0:T(4,128)S(1)}, u32[]{:S(2)}) copy-start(f32[4,256]{1,0:T(4,128)S(1)} %get-tuple-element.109) | copy-start | bytes 12292
  24.2 5.7 %copy-start.4 = (f32[4,256,256]{1,2,0:T(8,128)}, f32[4,256,256]{1,2,0:T(8,128)S(1)}, u32[]{:S(2)}) copy-start(f32[4,256,256]{1,2,0:T(8,128)S(1)} %get-tuple-element.116) | copy-start | bytes 3145732
  24.5 3.5 %copy-start.18 = (f32[4,256,256]{1,2,0:T(8,128)}, f32[4,256,256]{1,2,0:T(8,128)S(1)}, u32[]{:S(2)}) copy-start(f32[4,256,256]{1,2,0:T(8,128)S(1)} %get-tuple-element.94) | copy-start | bytes 3145732
  24.6 3.5 %copy-start.56 = (f32[4,256]{1,0:T(4,128)}, f32[4,256]{1,0:T(4,128)S(1)}, u32[]{:S(2)}) copy-start(f32[4,256]{1,0:T(4,128)S(1)} %get-tuple-element.93) | copy-start | bytes 12292
  24.9 5.0 %copy-start.6 = (f32[4,256,256]{1,2,0:T(8,128)}, f32[4,256,256]{1,2,0:T(8,128)S(1)}, u32[]{:S(2)}) copy-start(f32[4,256,256]{1,2,0:T(8,128)S(1)} %get-tuple-element.114) | copy-start | bytes 3145732
  24.9 4.9 %copy-start.44 = (f32[4,256]{1,0:T(4,128)}, f32[4,256]{1,0:T(4,128)S(1)}, u32[]{:S(2)}) copy-start(f32[4,256]{1,0:T(4,128)S(1)} %get-tuple-element.113) | copy-start | bytes 12292
  25.3 5.5 %copy-start.31 = (f32[4,256,256]{1,2,0:T(8,128)}, f32[4,256,256]{1,2,0:T(8,128)S(1)}, u32[]{:S(2)}) copy-start(f32[4,256,256]{1,2,0:T(8,128)S(1)} %get-tuple-element.118) | copy-start | bytes 3145732
  25.3 5.5 %copy-start.67 = (f32[4,256]{1,0:T(4,128)}, f32[4,256]{1,0:T(4,128)S(1)}, u32[]{:S(2)}) copy-start(f32[4,256]{1,0:T(4,128)S(1)} %get-tuple-element.117) | copy-start | bytes 12292
  38.5 3.6 %copy-start.22 = (f32[4,256,256]{1,2,0:T(8,128)}, f32[4,256,256]{1,2,0:T(8,128)S(1)}, u32[]{:S(2)}) copy-start(f32[4,256,256]{1,2,0:T(8,128)S(1)} %get-tuple-element.122) | copy-start | bytes 3145732
  38.5 3.6 %copy-start.60 = (f32[4,256]{1,0:T(4,128)}, f32[4,256]{1,0:T(4,128)S(1)}, u32[]{:S(2)}) copy-start(f32[4,256]{1,0:T(4,128)S(1)} %get-tuple-element.121) | copy-start | bytes 12292
  40.0 3.1 %copy-start.24 = (f32[4,256,256]{1,2,0:T(8,128)}, f32[4,256,256]{1,2,0:T(8,128)S(1)}, u32[]{:S(2)}) copy-start(f32[4,256,256]{1,2,0:T(8,128)S(1)} %get-tuple-element.120) | copy-start | bytes 3145732
  40.0 3.0 %copy-start.62 = (f32[4,256]{1,0:T(4,128)}, f32[4,256]{1,0:T(4,128)S(1)}, u32[]{:S(2)}) copy-start(f32[4,256]{1,0:T(4,128)S(1)} %get-tuple-element.119) | copy-start | bytes 12292
  48.9 7.4 %copy-start.41 = (bf16[256,256]{1,0:T(8,128)(2,1)S(1)}, bf16[256,256]{1,0:T(8,128)(2,1)}, u32[]{:S(2)}) copy-start(bf16[256,256]{1,0:T(8,128)(2,1)} %get-tuple-element.125) | copy-start | bytes 393220
  50.2 5.3 %copy-start.42 = (bf16[256,256]{1,0:T(8,128)(2,1)S(1)}, bf16[256,256]{1,0:T(8,128)(2,1)}, u32[]{:S(2)}) copy-start(bf16[256,256]{1,0:T(8,128)(2,1)} %get-tuple-element.124) | copy-start | bytes 393220
  59.2 12.0 %collective-permute-start.2 = (f32[2,4,256,64]{2,3,1,0:T(8,128)S(1)}, f32[2,4,256,64]{2,3,1,0:T(8,128)S(1)}, u32[]{:S(2)}, u32[]{:S(2)}) collective-permute-start(f32[2,4,256,64]{2,3,1,0:T(8,128)S(1)} %pad_maximum_fusion), channel_id=1, source_target_pairs={{0,4},{4,8},{8,12},{12,16},{16,20},{20,24},{24,28},{28,0},{1,5},{5... | collective-permute-start | bytes 1572872 | tf_op jit(solution)/shard_map/ppermute | solution.py:17
  59.3 9.5 %collective-permute-start.3 = (f32[2,4,256]{2,1,0:T(4,128)S(1)}, f32[2,4,256]{2,1,0:T(4,128)S(1)}, u32[]{:S(2)}, u32[]{:S(2)}) collective-permute-start(f32[2,4,256]{2,1,0:T(4,128)S(1)} %pad_maximum_fusion.2), channel_id=1, source_target_pairs={{0,4},{4,8},{8,12},{12,16},{16,20},{20,24},{24,28},{28,0},{1,5},{5... | collective-permute-start | bytes 24584 | tf_op jit(solution)/shard_map/ppermute | solution.py:17
  59.4 9.5 %collective-permute-start.1 = (f32[2,4,256]{2,1,0:T(4,128)S(1)}, f32[2,4,256]{2,1,0:T(4,128)S(1)}, u32[]{:S(2)}, u32[]{:S(2)}) collective-permute-start(f32[2,4,256]{2,1,0:T(4,128)S(1)} %pad_maximum_fusion.1), channel_id=1, source_target_pairs={{0,4},{4,8},{8,12},{12,16},{16,20},{20,24},{24,28},{28,0},{1,5},{5... | collective-permute-start | bytes 24584 | tf_op jit(solution)/shard_map/ppermute | solution.py:17
  64.5 4.4 %copy-start.45 = (f32[4,256]{1,0:T(4,128)S(1)}, f32[4,256]{1,0:T(4,128)}, u32[]{:S(2)}) copy-start(f32[4,256]{1,0:T(4,128)} %copy-done.44) | copy-start | bytes 12292
  64.5 4.4 %copy-start.66 = (f32[4,256]{1,0:T(4,128)S(1)}, f32[4,256]{1,0:T(4,128)}, u32[]{:S(2)}) copy-start(f32[4,256]{1,0:T(4,128)} %copy-done.65) | copy-start | bytes 12292
  64.5 4.4 %copy-start.73 = (f32[4,256]{1,0:T(4,128)S(1)}, f32[4,256]{1,0:T(4,128)}, u32[]{:S(2)}) copy-start(f32[4,256]{1,0:T(4,128)} %get-tuple-element.134) | copy-start | bytes 12292
  64.5 4.4 %copy-start.74 = (f32[4,256]{1,0:T(4,128)S(1)}, f32[4,256]{1,0:T(4,128)}, u32[]{:S(2)}) copy-start(f32[4,256]{1,0:T(4,128)} %get-tuple-element.135) | copy-start | bytes 12292
  64.6 4.4 %copy-start.75 = (f32[4,256]{1,0:T(4,128)S(1)}, f32[4,256]{1,0:T(4,128)}, u32[]{:S(2)}) copy-start(f32[4,256]{1,0:T(4,128)} %get-tuple-element.132) | copy-start | bytes 12292
  64.6 4.4 %copy-start.76 = (f32[4,256]{1,0:T(4,128)S(1)}, f32[4,256]{1,0:T(4,128)}, u32[]{:S(2)}) copy-start(f32[4,256]{1,0:T(4,128)} %get-tuple-element.133) | copy-start | bytes 12292
  64.6 4.4 %copy-start.7 = (f32[4,256,256]{1,2,0:T(8,128)S(1)}, f32[4,256,256]{1,2,0:T(8,128)}, u32[]{:S(2)}) copy-start(f32[4,256,256]{1,2,0:T(8,128)} %copy-done.6) | copy-start | bytes 3145732
  64.6 4.8 %copy-start.5 = (f32[4,256,256]{1,2,0:T(8,128)S(1)}, f32[4,256,256]{1,2,0:T(8,128)}, u32[]{:S(2)}) copy-start(f32[4,256,256]{1,2,0:T(8,128)} %copy-done.4) | copy-start | bytes 3145732
  65.1 4.6 %copy-start.3 = (f32[4,256,256]{1,2,0:T(8,128)S(1)}, f32[4,256,256]{1,2,0:T(8,128)}, u32[]{:S(2)}) copy-start(f32[4,256,256]{1,2,0:T(8,128)} %copy-done.2) | copy-start | bytes 3145732
  74.7 2.9 %copy-start.90 = (s32[2]{0:T(128)S(1)}, s32[2]{0:T(128)}, u32[]{:S(2)}) copy-start(s32[2]{0:T(128)} %constant.85) | copy-start | bytes 28
  74.7 3.0 %copy-start.89 = (s32[2]{0:T(128)S(1)}, s32[2]{0:T(128)}, u32[]{:S(2)}) copy-start(s32[2]{0:T(128)} %constant.88) | copy-start | bytes 28
  82.8 8.0 %all-to-all-start = ((s32[8,1,256]{2,1,0:T(1,128)}), s32[8,1,256]{2,1,0:T(1,128)S(1)}, u32[]{:S(2)}, u32[]{:S(2)}) async-start(s32[8,1,256]{2,1,0:T(1,128)} %bitcast.88), calls=%async_computation.1 | async-start | bytes 16384 | tf_op jit(solution)/shard_map/all_to_all | solution.py:148
  128.1 3.8 %copy-start.87 = (f32[1024]{0:T(1024)S(1)}, f32[1024]{0:T(1024)}, u32[]{:S(2)}) copy-start(f32[1024]{0:T(1024)} %param.15) | copy-start | bytes 12292
  128.1 19.2 %all-to-all-start.1 = ((bf16[8,256,256]{2,1,0:T(8,128)(2,1)}), bf16[8,256,256]{2,1,0:T(8,128)(2,1)S(1)}, u32[]{:S(2)}, u32[]{:S(2)}) async-start(bf16[8,256,256]{2,1,0:T(8,128)(2,1)} %bitcast.91), calls=%async_computation.2 | async-start | bytes 2097152 | tf_op jit(solution)/shard_map/all_to_all | solution.py:150
  (50 other events, 70.2 us)
Sparse Core Ops, SparseCore 0:
  74.8 43.0 reduce-scatter.1
where the time goes:
time: 162 us; the launch traced here: 161 us
  waiting for transfers between devices  50.6 us (31%)
  local copies, waits for them, and re-layouts  38.1 us (24%)
  matrix products  25.7 us (16%)
  between operations  19.7 us (12%)
  other arithmetic  16.3 us (10%)
  starting transfers between devices  10.9 us (7%)
    reduce_scatter x1, waiting for transfers between devices, per_device(): lax.psum_scatter(group_terms.astype(jnp.bfloat16), 'heads', scatter_dimen...  27 us
    dot_general x20, matrix products, partial_block(): jnp.einsum('qhd,khd->hqk', query_heads, key_heads, preferred_element_type...  15.8 us
    all_to_all x1, waiting for transfers between devices, per_device(): lax.all_to_all(row_values, 'views', split_axis=0, concat_axis=0, tiled=True)  15.4 us
    unnamed x183, local copies, waits for them, and re-layouts  11.7 us
    gather x1, local copies, waits for them, and re-layouts, per_device(): layer_out[lax.all_to_all(requests, 'views', split_axis=0, concat_axis=0,...  9.06 us
    reduce_sum x14, other arithmetic, partial_block(): totals = jnp.sum(weights, axis=-1)  8.04 us
    dot_general x20, matrix products, partial_block(): jnp.einsum('hqk,khd->hqd', weights.astype(jnp.bfloat16), value_heads, pre...  5.96 us
    gather x1, local copies, waits for them, and re-layouts, per_device(): fetched = replies[target_block, slot_index]  5.79 us
  transfers between devices with their start and end apart: 7, of which 5 were waited for; matrix products, arithmetic and copies ran while one was open for 19% of the time, Pallas kernels for 0%

commit v1 on v0

v1 whole, which is shorter than its diff:
```python
import functools

import jax
import jax.numpy as jnp
from jax import lax
from jax.experimental import pallas as pl
from jax.experimental.pallas import tpu as pltpu
from jax.sharding import PartitionSpec as P

HEAD_DIM = 64
LANES = 128

neg_large = -1e30
coupling = 0.5
epsilon = 1e-06

bf16 = jnp.bfloat16
f32 = jnp.float32


def cost(flops, bytes_accessed, transcendentals=0):
    return pl.CostEstimate(
        flops=int(flops), bytes_accessed=int(bytes_accessed), transcendentals=int(transcendentals)
    )


def dot(a, b):
    return jnp.dot(a, b, preferred_element_type=f32)


def whole(*shape):
    return pl.BlockSpec(shape, lambda *_: (0,) * len(shape))


SMEM_SPEC = pl.BlockSpec(memory_space=pltpu.SMEM)


def qkv_kernel(count, lats, gain_ref, w_ref, outs):
    scale = HEAD_DIM ** (-0.5)
    for i in range(count):
        wide = lats[i][0].astype(f32)
        mean_square = jnp.mean(wide * wide, axis=-1, keepdims=True)
        normed = (wide * lax.rsqrt(mean_square + epsilon) * gain_ref[...]).astype(bf16)
        keys = dot(normed, w_ref[1]).astype(bf16)
        outs[2 * i + 1][0] = keys
        values = dot(normed, w_ref[2])
        outs[2 * i + 1][1] = jnp.transpose(values).astype(bf16)
        queries = dot(normed, w_ref[0])
        outs[2 * i][...] = jnp.transpose(queries).astype(bf16) * jnp.asarray(scale, bf16)


def project_views(latents, gain, w_qkv, which):
    _, tokens, width = latents.shape
    sub = w_qkv.shape[2]
    count = len(which)

    def body(*refs):
        qkv_kernel(count, refs[:count], refs[count], refs[count + 1], refs[count + 2 :])

    in_specs = [pl.BlockSpec((1, tokens, width), functools.partial(lambda v, i: (v, 0, 0), v)) for v in which]
    in_specs += [whole(1, width), whole(3, width, sub)]
    out_shape, out_specs = [], []
    for _ in which:
        out_shape += [
            jax.ShapeDtypeStruct((sub, tokens), bf16),
            jax.ShapeDtypeStruct((2, tokens, sub), bf16),
        ]
        out_specs += [whole(sub, tokens), whole(2, tokens, sub)]
    outs = pl.pallas_call(
        body,
        grid=(1,),
        in_specs=in_specs,
        out_specs=out_specs,
        out_shape=out_shape,
        name="project_views",
        cost_estimate=cost(
            count * 6 * tokens * width * sub, count * tokens * (width + 3 * sub) * 2 + 6 * width * sub
        ),
    )(*([latents] * count), gain, w_qkv)
    return {v: (outs[2 * i], outs[2 * i + 1]) for i, v in enumerate(which)}


def head_scores(q_ref, k_ref, h):
    per = LANES // HEAD_DIM
    j, slot = h // per, h % per
    own = q_ref[h * HEAD_DIM : (h + 1) * HEAD_DIM, :]
    zero = jnp.zeros_like(own)
    padded = jnp.concatenate([own if s == slot else zero for s in range(per)], axis=0)
    return dot(k_ref[0, :, j * LANES : (j + 1) * LANES], padded)


def weighted(v_ref, weights, h):
    return dot(v_ref[1, h * HEAD_DIM : (h + 1) * HEAD_DIM, :], weights.astype(bf16))


def start_view(q_ref, kv_ref, acc_ref, stat_ref, heads):
    for h in range(heads):
        scores = head_scores(q_ref, kv_ref, h)
        top = jnp.max(scores, axis=0, keepdims=True)
        weights = jnp.exp(scores - top)
        stat_ref[h : h + 1, :] = top
        stat_ref[heads + h : heads + h + 1, :] = jnp.sum(weights, axis=0, keepdims=True)
        acc_ref[h * HEAD_DIM : (h + 1) * HEAD_DIM, :] = weighted(kv_ref, weights, h)


def add_view(q_ref, kv_ref, acc_ref, stat_ref, heads):
    for h in range(heads):
        scores = head_scores(q_ref, kv_ref, h)
        old = stat_ref[h : h + 1, :]
        top = jnp.maximum(old, jnp.max(scores, axis=0, keepdims=True))
        weights = jnp.exp(scores - top)
        fade = jnp.exp(old - top)
        stat_ref[h : h + 1, :] = top
        total = stat_ref[heads + h : heads + h + 1, :]
        stat_ref[heads + h : heads + h + 1, :] = total * fade + jnp.sum(weights, axis=0, keepdims=True)
        rows = slice(h * HEAD_DIM, (h + 1) * HEAD_DIM)
        acc_ref[rows, :] = acc_ref[rows, :] * fade + weighted(kv_ref, weights, h)


def attention_cost(tokens, sub, pairs):
    heads = sub // HEAD_DIM
    return cost(
        pairs * heads * tokens * tokens * 4 * LANES,
        pairs * tokens * sub * 8,
        pairs * heads * tokens * tokens,
    )


def local_attention(meta, intersection, blocks, local_views, window):
    q0, kv0 = blocks[0]
    sub, tokens = q0.shape
    heads = sub // HEAD_DIM
    views_total = intersection.shape[0]

    def body(meta_ref, inter_ref, *refs):
        qs, kvs = refs[:local_views], refs[local_views : 2 * local_views]
        acc, stat = refs[2 * local_views :]
        first = meta_ref[0] * local_views
        for v in range(local_views):
            start_view(qs[v], kvs[v], acc.at[v], stat.at[v], heads)
        for v in range(local_views):
            for o in range(window):
                t = v + o + 1
                if t < local_views:

                    @pl.when(inter_ref[first + v, o] > 0)
                    def _(v=v, t=t):
                        add_view(qs[v], kvs[t], acc.at[v], stat.at[v], heads)
                        add_view(qs[t], kvs[v], acc.at[t], stat.at[t], heads)

    pairs = local_views * (2 * window + 1) - window * (window + 1)
    return pl.pallas_call(
        body,
        grid=(1,),
        in_specs=[SMEM_SPEC, SMEM_SPEC]
        + [whole(sub, tokens)] * local_views
        + [whole(2, tokens, sub)] * local_views,
        out_specs=[whole(local_views, sub, tokens), whole(local_views, 2 * heads, tokens)],
        out_shape=[
            jax.ShapeDtypeStruct((local_views, sub, tokens), f32),
            jax.ShapeDtypeStruct((local_views, 2 * heads, tokens), f32),
        ],
        name="local_attention",
        cost_estimate=attention_cost(tokens, sub, pairs),
    )(
        meta,
        intersection,
        *[blocks[v][0] for v in range(local_views)],
        *[blocks[v][1] for v in range(local_views)],
    )


def finish_attention(meta, intersection, acc, stat, local_views, plan, queries, remote):
    _, sub, tokens = acc.shape
    heads = sub // HEAD_DIM
    views_total = intersection.shape[0]
    names = sorted(remote)
    count = len(plan)

    def body(meta_ref, inter_ref, *refs):
        accs, stats = refs[:count], refs[count : 2 * count]
        qs = refs[2 * count : 3 * count]
        kvs = dict(zip(names, refs[3 * count : 3 * count + len(names)]))
        out, work, work_stat = refs[3 * count + len(names) :]
        first = meta_ref[0] * local_views
        for i, (view, sources) in enumerate(plan):
            work[i] = accs[i][0]
            work_stat[i] = stats[i][0]
            for name, source, offset in sources:
                at = first + source
                if source < 0:
                    at = jnp.where(at < 0, at + views_total, at)

                @pl.when(inter_ref[at, offset] > 0)
                def _(i=i, name=name):
                    add_view(qs[i], kvs[name], work.at[i], work_stat.at[i], heads)

        for i in range(count):
            parts = []
            for h in range(heads):
                total = work_stat[i, heads + h : heads + h + 1, :]
                parts.append(work[i, h * HEAD_DIM : (h + 1) * HEAD_DIM, :] / total)
            out[i] = jnp.transpose(jnp.concatenate(parts, axis=0)).astype(bf16)

    def view_spec(shape, v):
        return pl.BlockSpec((1,) + shape, lambda i: (v, 0, 0))

    pairs = sum(len(s) for _, s in plan)
    return pl.pallas_call(
        body,
        grid=(1,),
        in_specs=[SMEM_SPEC, SMEM_SPEC]
        + [view_spec((sub, tokens), v) for v, _ in plan]
        + [view_spec((2 * heads, tokens), v) for v, _ in plan]
        + [whole(sub, tokens)] * count
        + [whole(2, tokens, sub)] * len(names),
        out_specs=whole(count, tokens, sub),
        out_shape=jax.ShapeDtypeStruct((count, tokens, sub), bf16),
        scratch_shapes=[
            pltpu.VMEM((count, sub, tokens), f32),
            pltpu.VMEM((count, 2 * heads, tokens), f32),
        ],
        name="finish_attention",
        cost_estimate=attention_cost(tokens, sub, pairs),
    )(meta, intersection, *([acc] * count), *([stat] * count), *queries, *[remote[n] for n in names])


def project_out(meta, attended, weights, latents, view_of):
    count, tokens, sub = attended[0].shape
    groups = len(attended)

    def body(meta_ref, *refs):
        att, ws = refs[:groups], refs[groups : 2 * groups]
        lat, own, other = refs[2 * groups :]
        total = None
        for a, w in zip(att, ws):
            part = dot(a[0], w[...]).astype(bf16).astype(f32)
            total = part if total is None else total + part
        layer = (lat[0].astype(f32) + total).astype(bf16)
        low, high = layer[:, :sub], layer[:, sub:]
        odd = lax.rem(meta_ref[1], 2) == 1
        own[0] = jnp.where(odd, high, low)
        other[0] = jnp.where(odd, low, high)

    att_spec = pl.BlockSpec((1, tokens, sub), lambda i, m: (i, 0, 0))
    return pl.pallas_call(
        body,
        grid_spec=pltpu.PrefetchScalarGridSpec(
            num_scalar_prefetch=1,
            grid=(count,),
            in_specs=[att_spec] * groups
            + [whole(sub, 2 * sub)] * groups
            + [pl.BlockSpec((1, tokens, 2 * sub), lambda i, m: (view_of(i), 0, m[1] // 2))],
            out_specs=[att_spec, att_spec],
        ),
        out_shape=[jax.ShapeDtypeStruct((count, tokens, sub), bf16)] * 2,
        name="project_out",
        cost_estimate=cost(
            groups * count * tokens * sub * 4 * sub,
            groups * (count * tokens * sub + 2 * sub * sub) * 2 + count * tokens * sub * 8,
        ),
    )(meta, *attended, *weights, latents)


def prepare_requests(block_rows, token_rows, peers, capacity):
    strips, lanes = block_rows.shape

    def body(block_ref, token_ref, wanted_ref, code_ref):
        before = (
            lax.broadcasted_iota(jnp.int32, (lanes, lanes), 0)
            < lax.broadcasted_iota(jnp.int32, (lanes, lanes), 1)
        ).astype(bf16)
        peer_ids = lax.broadcasted_iota(jnp.int32, (peers, lanes), 0)
        carry = jnp.zeros((peers, 1), f32)
        slots, lefts = [], []
        for i in range(strips):
            block = block_ref[i : i + 1, :]
            hit = (peer_ids == block).astype(f32)
            rank = dot(hit.astype(bf16), before) + carry
            carry = carry + jnp.sum(hit, axis=1, keepdims=True)
            slot = jnp.sum(rank * hit, axis=0, keepdims=True)
            slots.append(slot)
            code_ref[i : i + 1, :] = block * capacity + slot.astype(jnp.int32)
            token = token_ref[i : i + 1, :]
            coarse = (token // 32).astype(f32)
            fine = (token % 32).astype(f32)
            lefts.append(jnp.concatenate([hit * coarse, hit * fine], axis=0).astype(bf16))
        columns = jnp.transpose(jnp.concatenate(slots, axis=0))
        place = lax.broadcasted_iota(jnp.int32, (lanes, capacity), 1).astype(f32)
        total = jnp.zeros((2 * peers, capacity), f32)
        for i in range(strips):
            spot = (columns[:, i : i + 1] == place).astype(bf16)
            total = total + dot(lefts[i], spot)
        wanted_ref[...] = (total[:peers] * 32.0 + total[peers:]).astype(jnp.int32)

    return pl.pallas_call(
        body,
        out_shape=[
            jax.ShapeDtypeStruct((peers, capacity), jnp.int32),
            jax.ShapeDtypeStruct((strips, lanes), jnp.int32),
        ],
        name="prepare_requests",
        cost_estimate=cost(2 * strips * lanes * lanes * capacity, 3 * strips * lanes * 4),
    )(block_rows, token_rows)


def gather_rows(meta, wanted, pieces, place_of):
    peers, capacity = wanted.shape
    _, tokens, sub = pieces[0][0].shape
    local_views = len(place_of)
    rows = local_views * tokens
    flat = [p for pair in pieces for p in pair]

    def body(meta_ref, wanted_ref, *refs):
        ins = refs[: len(flat)]
        layer, outs = refs[len(flat)], refs[len(flat) + 1 :]
        end = jnp.logical_or(meta_ref[1] == 0, meta_ref[1] == meta_ref[2] - 1)
        for v, (c, i) in enumerate(place_of):
            layer[v * tokens : (v + 1) * tokens, :] = jnp.where(
                end, ins[2 * c + 1][i], ins[2 * c][i]
            )
        full = layer[...]
        row_ids = lax.broadcasted_iota(jnp.int32, (capacity, rows), 1)
        for mask in range(peers):
            peer = lax.bitwise_xor(meta_ref[0], mask)
            line = wanted_ref[pl.ds(peer, 1), :]
            column = jnp.transpose(jnp.broadcast_to(line, (8, capacity)))[:, :1]
            pick = jnp.where(column == row_ids, 1.0, 0.0).astype(bf16)
            outs[mask][...] = dot(pick, full).astype(bf16)

    return pl.pallas_call(
        body,
        grid=(1,),
        in_specs=[SMEM_SPEC, whole(peers, capacity)] + [whole(*p.shape) for p in flat],
        out_specs=[whole(rows, sub)] + [whole(capacity, sub)] * peers,
        out_shape=[jax.ShapeDtypeStruct((rows, sub), bf16)]
        + [jax.ShapeDtypeStruct((capacity, sub), bf16)] * peers,
        name="gather_rows",
        cost_estimate=cost(2 * peers * capacity * rows * sub, 2 * (rows + peers * capacity) * sub * 2),
    )(meta, wanted, *flat)


def finish_rows(meta, code, confidence, layer, replies, tokens):
    rows, sub = layer.shape
    peers = len(replies)
    capacity = replies[0].shape[0]
    strips, lanes = code.shape
    blocks = rows // tokens
    per = tokens // lanes

    def column_of(rows_ref, g):
        turned = jnp.transpose(rows_ref[...].astype(f32))
        lane = lax.broadcasted_iota(jnp.int32, turned.shape, 1)
        parts = [
            jnp.sum(jnp.where(lane == g * per + j, turned, 0.0), axis=1, keepdims=True)
            for j in range(per)
        ]
        return jnp.concatenate(parts, axis=0)

    def body(meta_ref, code_ref, conf_ref, layer_ref, *refs):
        reps, out = refs[:peers], refs[peers]
        g = pl.program_id(0)
        codes = column_of(code_ref, g)
        weight = column_of(conf_ref, g) * coupling
        place = lax.broadcasted_iota(jnp.int32, (tokens, capacity), 1).astype(f32)
        fetched = None
        for mask in range(peers):
            peer = lax.bitwise_xor(meta_ref[0], mask)
            shifted = codes - (peer * capacity).astype(f32)
            pick = jnp.where(shifted == place, 1.0, 0.0).astype(bf16)
            part = dot(pick, reps[mask][...])
            fetched = part if fetched is None else fetched + part
        wide = layer_ref[...].astype(f32)
        out[...] = wide + weight * (fetched - wide)

    row_spec = pl.BlockSpec((tokens, sub), lambda g: (g, 0))
    return pl.pallas_call(
        body,
        grid=(blocks,),
        in_specs=[SMEM_SPEC, whole(strips, lanes), whole(strips, lanes), row_spec]
        + [whole(capacity, sub)] * peers,
        out_specs=row_spec,
        out_shape=jax.ShapeDtypeStruct((rows, sub), f32),
        name="finish_rows",
        cost_estimate=cost(2 * peers * capacity * rows * sub, rows * sub * 6 + peers * capacity * sub * 2),
    )(meta, code, confidence, layer, *replies)


def per_device(latents, norm_gain, w_qkv, w_out, intersection, match_block, match_row, confidence):
    local_views, tokens, width = latents.shape
    window = intersection.shape[1]
    sub = w_qkv.shape[2]
    peers = lax.axis_size("views")
    ends = lax.axis_size("heads")
    rows = local_views * tokens
    capacity = 2 * rows // peers
    assert local_views == 4 and window == 2 and ends == 4 and tokens == sub
    view_at, head_at = lax.axis_index("views"), lax.axis_index("heads")
    spot = jnp.arange(4, dtype=jnp.int32)
    meta = jnp.where(spot == 0, view_at, jnp.where(spot == 1, head_at, ends)).astype(jnp.int32)

    def along(x, by):
        return lax.ppermute(x, "views", [(i, (i + by) % peers) for i in range(peers)])

    def across(x, pairs):
        return lax.ppermute(x, "heads", pairs)

    beside, middle, beyond, back = (
        [(0, 1), (3, 2)],
        [(1, 2), (2, 1)],
        [(0, 2), (3, 1)],
        [(1, 0), (2, 3)],
    )
    gain = norm_gain.reshape(1, width)
    blocks = project_views(latents, gain, w_qkv, (0, local_views - 1))
    next_first = along(blocks[0][1], -1)
    prev_last = along(blocks[3][1], 1)
    blocks.update(project_views(latents, gain, w_qkv, (1, 2)))
    next_second = along(blocks[1][1], -1)
    prev_second = along(blocks[2][1], 1)

    half = 2 * sub
    low_end = head_at // 2
    own_half = lax.dynamic_slice_in_dim(w_out, low_end * half, half, 1)
    other_half = lax.dynamic_slice_in_dim(w_out, (1 - low_end) * half, half, 1)
    weights = [
        own_half,
        across(own_half, beside),
        across(other_half, middle),
        across(other_half, beyond),
    ]

    strips = rows // LANES
    wanted, code = prepare_requests(
        match_block.reshape(strips, LANES), match_row.reshape(strips, LANES), peers, capacity
    )
    wanted = lax.all_to_all(wanted, "views", split_axis=0, concat_axis=0, tiled=True)

    acc, stat = local_attention(meta, intersection, blocks, local_views, window)
    finish = functools.partial(finish_attention, meta, intersection, acc, stat, local_views)
    inner = finish(
        [(1, [("prev_last", -1, 1)]), (2, [("next_first", 2, 1)])],
        [blocks[1][0], blocks[2][0]],
        dict(prev_last=prev_last, next_first=next_first),
    )
    outer = finish(
        [
            (0, [("prev_last", -1, 0), ("prev_second", -2, 1)]),
            (3, [("next_first", 3, 0), ("next_second", 3, 1)]),
        ],
        [blocks[0][0], blocks[3][0]],
        dict(
            prev_last=prev_last,
            next_first=next_first,
            prev_second=prev_second,
            next_second=next_second,
        ),
    )
    pieces = []
    for chunk, view_of in ((inner, lambda i: i + 1), (outer, lambda i: 3 * i)):
        attended = [chunk, across(chunk, beside), across(chunk, middle), across(chunk, beyond)]
        own, other = project_out(meta, attended, weights, latents, view_of)
        pieces.append((own, across(other, back)))

    place_of = [(1, 0), (0, 0), (0, 1), (1, 1)]
    layer, *outgoing = gather_rows(meta, wanted, pieces, place_of)
    replies = [outgoing[0]]
    for mask in range(1, peers):
        replies.append(lax.ppermute(outgoing[mask], "views", [(i, i ^ mask) for i in range(peers)]))
    refined = finish_rows(
        meta, code, confidence.reshape(strips, LANES), layer, replies, tokens
    )
    return refined.reshape(local_views, tokens, sub)


def solution(mesh):
    in_specs = (
        P("views", None, None),
        P(),
        P(None, None, "heads"),
        P("heads", None),
        P(),
        P("views", None),
        P("views"),
        P("views"),
    )
    out_specs = P("views", None, "heads")
    return jax.shard_map(
        per_device, mesh=mesh, in_specs=in_specs, out_specs=out_specs, check_vma=False
    )
```

time: 162 us -> 112 us (0.69)
  Pallas kernels: 0 us -> 50 us
  waiting for transfers between devices: 50.6 us -> 11.4 us
  local copies, waits for them, and re-layouts: 38.1 us -> 7.14 us
  matrix products: 25.7 us -> 0 us
  starting transfers between devices: 10.9 us -> 31.9 us
  between operations: 19.7 us -> 0.42 us
  other arithmetic: 16.3 us -> 0.52 us
  blocking collectives: 0 us -> 9.6 us
    pallas_call x0 -> x10, Pallas kernels: none -> 50 us  [the longest x1 15.6 us: local_attention(): pl.pallas_call(body, grid=(1,), in_specs=[SMEM_SPEC, SMEM_SPEC] + [whole(...]
    ppermute x4 -> x22, starting transfers between devices: 3.76 us -> 31.9 us  [the longest x11 21.7 us: across(): return lax.ppermute(x, 'heads', pairs)]
    reduce_scatter x1 -> x0, waiting for transfers between devices: 27 us -> none  [per_device(): lax.psum_scatter(group_terms.astype(jnp.bfloat16), 'heads', scatter_dimen...]
    dot_general x42 -> x0, matrix products: 25.7 us -> none  [the longest x20 15.8 us: partial_block(): jnp.einsum('qhd,khd->hqk', query_heads, key_heads, preferred_element_type...]
    all_to_all x2 -> x0, waiting for transfers between devices: 20 us -> none  [the longest x1 15.4 us: per_device(): lax.all_to_all(row_values, 'views', split_axis=0, concat_axis=0, tiled=True)]
    gather x2 -> x0, local copies, waits for them, and re-layouts: 14.9 us -> none  [the longest x1 9.06 us: per_device(): layer_out[lax.all_to_all(requests, 'views', split_axis=0, concat_axis=0,...]
    reduce_sum x16 -> x0, other arithmetic: 10.3 us -> none  [the longest x14 8.04 us: partial_block(): totals = jnp.sum(weights, axis=-1)]
    all_to_all x0 -> x1, blocking collectives: none -> 9.6 us  [per_device(): lax.all_to_all(wanted, 'views', split_axis=0, concat_axis=0, tiled=True)]
  transfers between devices with their start and end apart: 7 -> 22, of which waited for: 5 -> 3; matrix products, arithmetic and copies ran while one was open for 19% -> 2% of each run, Pallas kernels for 0% -> 34%
where the time goes in v1:
time: 112 us; the launch traced here: 111 us
  Pallas kernels  50 us (45%)
  starting transfers between devices  31.9 us (28%)
  waiting for transfers between devices  11.4 us (10%)
  blocking collectives  9.6 us (9%)
  local copies, waits for them, and re-layouts  7.14 us (6%)
    ppermute x11, starting transfers between devices, across(): return lax.ppermute(x, 'heads', pairs)  21.7 us
    pallas_call x1, Pallas kernels, local_attention(): pl.pallas_call(body, grid=(1,), in_specs=[SMEM_SPEC, SMEM_SPEC] + [whole(...  15.6 us
    ppermute x7, waiting for transfers between devices, per_device(): lax.ppermute(outgoing[mask], 'views', [(i, i ^ mask) for i in range(peers)])  11.3 us
    all_to_all x1, blocking collectives, per_device(): lax.all_to_all(wanted, 'views', split_axis=0, concat_axis=0, tiled=True)  9.6 us
    pallas_call x2, Pallas kernels, finish_attention(): pl.pallas_call(body, grid=(1,), in_specs=[SMEM_SPEC, SMEM_SPEC] + [view_s...  8.25 us
    pallas_call x2, Pallas kernels, project_out(): pl.pallas_call(body, grid_spec=pltpu.PrefetchScalarGridSpec(num_scalar_pr...  8.09 us
    pallas_call x2, Pallas kernels, project_views(): pl.pallas_call(body, grid=(1,), in_specs=in_specs, out_specs=out_specs, o...  7.4 us
    unnamed x52, local copies, waits for them, and re-layouts  6.39 us
  transfers between devices with their start and end apart: 22, of which 3 were waited for; matrix products, arithmetic and copies ran while one was open for 2% of the time, Pallas kernels for 34%

profile of v1, /device:TPU:0, one launch (start us, length us, event | category | flops | bytes accessed | tf_op | source)
XLA Modules:
  0.0 110.9 jit_solution(18047424739318277914)
XLA Ops:
  0.0 3.7 %project_views.2 = (bf16[256,256]{1,0:T(8,128)(2,1)}, bf16[2,256,256]{2,1,0:T(8,128)(2,1)}, bf16[256,256]{1,0:T(8,128)(2,1)}, bf16[2,256,256]{2,1,0:T(8,128)(2,1)}) custom-call(bf16[4,256,1024]{2,1,0:T(8,128)(2,1)} %refs_8_.3, bf16[4,256,1024]{2,1,0:T(8,128)(2,1)} %refs_8_.3, f32[1,1024]{1,0:T(1,128)} %bitcast.9, bf16[3,1024,256]{2,1,0:T(8,128)(2,1)} %refs_3_.3), custom_call_target="tpu_custom_call" | custom-call | flops 805306368 | bytes 3407872 | tf_op jit(solution)/shard_map/project_views/pallas_call | solution.py:69
  3.7 3.4 %collective-permute-start = (bf16[2,256,256]{2,1,0:T(8,128)(2,1)}, bf16[2,256,256]{2,1,0:T(8,128)(2,1)S(1)}, u32[]{:S(2)}, u32[]{:S(2)}) collective-permute-start(bf16[2,256,256]{2,1,0:T(8,128)(2,1)} %get-tuple-element.36.refs_4_), channel_id=1, source_target_pairs={{0,28},{4,0},{8,4},{12,8},{16,12},{20,16},{24,20},{28,24},{1,29},{... | collective-permute-start | bytes 786440 | tf_op jit(solution)/shard_map/ppermute | solution.py:403
  7.1 3.7 %project_views.3 = (bf16[256,256]{1,0:T(8,128)(2,1)}, bf16[2,256,256]{2,1,0:T(8,128)(2,1)}, bf16[256,256]{1,0:T(8,128)(2,1)}, bf16[2,256,256]{2,1,0:T(8,128)(2,1)}) custom-call(bf16[4,256,1024]{2,1,0:T(8,128)(2,1)} %refs_8_.3, bf16[4,256,1024]{2,1,0:T(8,128)(2,1)} %refs_8_.3, f32[1,1024]{1,0:T(1,128)} %bitcast.10, bf16[3,1024,256]{2,1,0:T(8,128)(2,1)} %refs_3_.3), custom_call_target="tpu_custom_call" | custom-call | flops 805306368 | bytes 3407872 | tf_op jit(solution)/shard_map/project_views/pallas_call | solution.py:69
  10.8 2.6 %collective-permute-start.9 = (bf16[2,256,256]{2,1,0:T(8,128)(2,1)}, bf16[2,256,256]{2,1,0:T(8,128)(2,1)S(1)}, u32[]{:S(2)}, u32[]{:S(2)}) collective-permute-start(bf16[2,256,256]{2,1,0:T(8,128)(2,1)} %get-tuple-element.37.refs_5_), channel_id=1, source_target_pairs={{0,28},{4,0},{8,4},{12,8},{16,12},{20,16},{24,20},{28,24},{1,29},{... | collective-permute-start | bytes 786440 | tf_op jit(solution)/shard_map/ppermute | solution.py:403
  13.5 3.5 %collective-permute-start.5 = (bf16[256,512]{1,0:T(8,128)(2,1)S(1)}, bf16[256,512]{1,0:T(8,128)(2,1)S(1)}, u32[]{:S(2)}, u32[]{:S(2)}) collective-permute-start(bf16[256,512]{1,0:T(8,128)(2,1)S(1)} %get-tuple-element.56.refs_4_), channel_id=1, source_target_pairs={{0,1},{3,2},{4,5},{7,6},{8,9},{11,10},{12,13},{15,14},{16,17},{19,... | collective-permute-start | bytes 786440 | tf_op jit(solution)/shard_map/ppermute | solution.py:406
  17.0 0.7 copy.14.inter_ref
  17.7 0.5 compare_select_fusion.1.meta_ref
  18.2 15.6 %local_attention.1 = (f32[4,256,256]{2,1,0:T(8,128)}, f32[4,8,256]{2,1,0:T(8,128)}) custom-call(s32[4]{0:T(128)} %compare_select_fusion.1.meta_ref, s32[32,2]{1,0:T(8,128)} %copy.14.inter_ref, bf16[256,256]{1,0:T(8,128)(2,1)} %get-tuple-element.32.refs_0_.refs_4_, bf16[256,256]{1,0:T(8,128)(2,1)} %get-tuple-element.33.refs_1_.refs_4_, ...), custom_call_target="tpu_custom_call" | custom-call | flops 1879048192 | bytes 7340032 | tf_op jit(solution)/shard_map/local_attention/pallas_call | solution.py:152
  33.8 0.7 collective-permute-start.6
  34.5 4.0 %collective-permute-start.7 = (bf16[256,512]{1,0:T(8,128)(2,1)S(1)}, bf16[256,512]{1,0:T(8,128)(2,1)S(1)}, u32[]{:S(2)}, u32[]{:S(2)}) collective-permute-start(bf16[256,512]{1,0:T(8,128)(2,1)S(1)} %get-tuple-element.55), channel_id=1, source_target_pairs={{0,2},{3,1},{4,6},{7,5},{8,10},{11,9},{12,14},{15,13},{16,18},{19,... | collective-permute-start | bytes 786440 | tf_op jit(solution)/shard_map/ppermute | solution.py:406
  38.5 0.7 copy-done.7
  39.2 0.1 copy-done.8
  39.3 4.9 %finish_attention.3.refs_0_ = bf16[2,256,256]{2,1,0:T(8,128)(2,1)} custom-call(s32[4]{0:T(128)} %compare_select_fusion.1.meta_ref, s32[32,2]{1,0:T(8,128)} %copy.14.inter_ref, f32[4,256,256]{2,1,0:T(8,128)} %get-tuple-element.40.refs_0_.refs_1_, f32[4,256,256]{2,1,0:T(8,128)} %get-tuple-element.40.refs_0_.refs_1_, ...), custom_call_target="tpu_custom_call" | custom-call | flops 536870912 | bytes 2097152 | tf_op jit(solution)/shard_map/finish_attention/pallas_call | solution.py:209
  44.2 1.4 %collective-permute-start.11 = (bf16[2,256,256]{2,1,0:T(8,128)(2,1)}, bf16[2,256,256]{2,1,0:T(8,128)(2,1)S(1)}, u32[]{:S(2)}, u32[]{:S(2)}) collective-permute-start(bf16[2,256,256]{2,1,0:T(8,128)(2,1)} %finish_attention.3.refs_0_), channel_id=1, source_target_pairs={{0,1},{3,2},{4,5},{7,6},{8,9},{11,10},{12,13},{15,14},{16,17},{19,... | collective-permute-start | bytes 786440 | tf_op jit(solution)/shard_map/ppermute | solution.py:406
  45.6 0.7 collective-permute-start.12
  46.3 4.0 %collective-permute-start.13 = (bf16[2,256,256]{2,1,0:T(8,128)(2,1)}, bf16[2,256,256]{2,1,0:T(8,128)(2,1)S(1)}, u32[]{:S(2)}, u32[]{:S(2)}) collective-permute-start(bf16[2,256,256]{2,1,0:T(8,128)(2,1)} %finish_attention.3.refs_0_), channel_id=1, source_target_pairs={{0,2},{3,1},{4,6},{7,5},{8,10},{11,9},{12,14},{15,13},{16,18},{19,... | collective-permute-start | bytes 786440 | tf_op jit(solution)/shard_map/ppermute | solution.py:406
  50.3 3.4 %finish_attention.2.refs_0_ = bf16[2,256,256]{2,1,0:T(8,128)(2,1)} custom-call(s32[4]{0:T(128)} %compare_select_fusion.1.meta_ref, s32[32,2]{1,0:T(8,128)} %copy.14.inter_ref, f32[4,256,256]{2,1,0:T(8,128)} %get-tuple-element.40.refs_0_.refs_1_, f32[4,256,256]{2,1,0:T(8,128)} %get-tuple-element.40.refs_0_.refs_1_, ...), custom_call_target="tpu_custom_call" | custom-call | flops 268435456 | bytes 1048576 | tf_op jit(solution)/shard_map/finish_attention/pallas_call | solution.py:209
  53.7 1.3 %collective-permute-start.2 = (bf16[2,256,256]{2,1,0:T(8,128)(2,1)}, bf16[2,256,256]{2,1,0:T(8,128)(2,1)S(1)}, u32[]{:S(2)}, u32[]{:S(2)}) collective-permute-start(bf16[2,256,256]{2,1,0:T(8,128)(2,1)} %finish_attention.2.refs_0_), channel_id=1, source_target_pairs={{0,1},{3,2},{4,5},{7,6},{8,9},{11,10},{12,13},{15,14},{16,17},{19,... | collective-permute-start | bytes 786440 | tf_op jit(solution)/shard_map/ppermute | solution.py:406
  55.0 0.7 collective-permute-start.3
  55.7 3.0 %collective-permute-start.4 = (bf16[2,256,256]{2,1,0:T(8,128)(2,1)}, bf16[2,256,256]{2,1,0:T(8,128)(2,1)S(1)}, u32[]{:S(2)}, u32[]{:S(2)}) collective-permute-start(bf16[2,256,256]{2,1,0:T(8,128)(2,1)} %finish_attention.2.refs_0_), channel_id=1, source_target_pairs={{0,2},{3,1},{4,6},{7,5},{8,10},{11,9},{12,14},{15,13},{16,18},{19,... | collective-permute-start | bytes 786440 | tf_op jit(solution)/shard_map/ppermute | solution.py:406
  58.8 0.7 copy-done.11
  59.4 0.7 copy-done.12
  60.1 4.0 %project_out.3 = (bf16[2,256,256]{2,1,0:T(8,128)(2,1)}, bf16[2,256,256]{2,1,0:T(8,128)(2,1)}) custom-call(s32[4]{0:T(128)} %compare_select_fusion.1.meta_ref, bf16[2,256,256]{2,1,0:T(8,128)(2,1)} %finish_attention.3.refs_0_, bf16[2,256,256]{2,1,0:T(8,128)(2,1)} %copy-done.9, bf16[2,256,256]{2,1,0:T(8,128)(2,1)} %copy-done.11, ...), custom_call_target="tpu_custom_call" | custom-call | flops 536870912 | bytes 3145728 | tf_op jit(solution)/shard_map/project_out/pallas_call | solution.py:246
  64.2 1.3 %collective-permute-start.14 = (bf16[2,256,256]{2,1,0:T(8,128)(2,1)}, bf16[2,256,256]{2,1,0:T(8,128)(2,1)S(1)}, u32[]{:S(2)}, u32[]{:S(2)}) collective-permute-start(bf16[2,256,256]{2,1,0:T(8,128)(2,1)} %get-tuple-element.45), channel_id=1, source_target_pairs={{1,0},{2,3},{5,4},{6,7},{9,8},{10,11},{13,12},{14,15},{17,16},{18,... | collective-permute-start | bytes 786440 | tf_op jit(solution)/shard_map/ppermute | solution.py:406
  65.5 0.7 copy-done.10
  66.2 0.1 copy-done.13
  66.2 0.7 copy-done.14
  66.9 4.1 %project_out.2 = (bf16[2,256,256]{2,1,0:T(8,128)(2,1)}, bf16[2,256,256]{2,1,0:T(8,128)(2,1)}) custom-call(s32[4]{0:T(128)} %compare_select_fusion.1.meta_ref, bf16[2,256,256]{2,1,0:T(8,128)(2,1)} %finish_attention.2.refs_0_, bf16[2,256,256]{2,1,0:T(8,128)(2,1)} %copy-done.10, bf16[2,256,256]{2,1,0:T(8,128)(2,1)} %copy-done.13, ...), custom_call_target="tpu_custom_call" | custom-call | flops 536870912 | bytes 3145728 | tf_op jit(solution)/shard_map/project_out/pallas_call | solution.py:246
  71.0 1.3 %collective-permute-start.8 = (bf16[2,256,256]{2,1,0:T(8,128)(2,1)}, bf16[2,256,256]{2,1,0:T(8,128)(2,1)S(1)}, u32[]{:S(2)}, u32[]{:S(2)}) collective-permute-start(bf16[2,256,256]{2,1,0:T(8,128)(2,1)} %get-tuple-element.43), channel_id=1, source_target_pairs={{1,0},{2,3},{5,4},{6,7},{9,8},{10,11},{13,12},{14,15},{17,16},{18,... | collective-permute-start | bytes 786440 | tf_op jit(solution)/shard_map/ppermute | solution.py:406
  72.3 2.0 %prepare_requests.1 = (s32[8,256]{1,0:T(8,128)}, s32[8,128]{1,0:T(8,128)}) custom-call(s32[8,128]{1,0:T(8,128)} %bitcast.13, s32[8,128]{1,0:T(8,128)} %bitcast.14), custom_call_target="tpu_custom_call" | custom-call | flops 67108864 | bytes 12288 | tf_op jit(solution)/shard_map/prepare_requests/pallas_call | solution.py:296
  74.3 0.7 copy.12
  75.0 9.6 %all_to_all.11 = s32[8,1,256]{2,1,0:T(1,128)S(1)} all-to-all(s32[8,1,256]{2,1,0:T(1,128)S(1)} %copy.12), channel_id=1, replica_groups=mesh['views'=8,'heads'=4] {'views'}, dimensions={0} | all-to-all | bytes 16384 | tf_op jit(solution)/shard_map/all_to_all | solution.py:437
  84.6 0.6 copy.18
  85.2 0.7 copy-done.16
  85.9 0.1 copy-done.17
  86.0 3.4 %gather_rows.1 = (bf16[1024,256]{1,0:T(8,128)(2,1)}, bf16[256,256]{1,0:T(8,128)(2,1)}, bf16[256,256]{1,0:T(8,128)(2,1)}, bf16[256,256]{1,0:T(8,128)(2,1)}, bf16[...) custom-call(s32[4]{0:T(128)} %compare_select_fusion.1.meta_ref, ...), custom_call_target="tpu_custom_call" | custom-call | flops 1073741824 | bytes 3145728 | tf_op jit(solution)/shard_map/gather_rows/pallas_call | solution.py:331
  89.4 0.7 collective-permute-start.16
  90.0 1.2 %collective-permute-start.17 = (bf16[256,256]{1,0:T(8,128)(2,1)}, bf16[256,256]{1,0:T(8,128)(2,1)S(1)}, u32[]{:S(2)}, u32[]{:S(2)}) collective-permute-start(bf16[256,256]{1,0:T(8,128)(2,1)} %get-tuple-element.50), channel_id=1, source_target_pairs={{0,12},{4,8},{8,4},{12,0},{16,28},{20,24},{24,20},{28,16},{1,13},{... | collective-permute-start | bytes 393224 | tf_op jit(solution)/shard_map/ppermute | solution.py:469
  91.2 0.6 collective-permute-start.18
  91.8 1.1 collective-permute-start.19
  92.9 0.7 collective-permute-start.20
  93.5 2.4 %collective-permute-done.16.refs_2_ = bf16[256,256]{1,0:T(8,128)(2,1)S(1)} collective-permute-done((bf16[256,256]{1,0:T(8,128)(2,1)}, bf16[256,256]{1,0:T(8,128)(2,1)S(1)}, u32[]{:S(2)}, u32[]{:S(2)}) %collective-permute-start.16) | collective-permute-done | bytes 131104 | tf_op jit(solution)/shard_map/ppermute | solution.py:469
  95.9 1.9 %collective-permute-done.17.refs_3_ = bf16[256,256]{1,0:T(8,128)(2,1)S(1)} collective-permute-done((bf16[256,256]{1,0:T(8,128)(2,1)}, bf16[256,256]{1,0:T(8,128)(2,1)S(1)}, u32[]{:S(2)}, u32[]{:S(2)}) %collective-permute-start.17) | collective-permute-done | bytes 131104 | tf_op jit(solution)/shard_map/ppermute | solution.py:469
  97.9 7.0 %collective-permute-done.19.refs_5_ = bf16[256,256]{1,0:T(8,128)(2,1)S(1)} collective-permute-done((bf16[256,256]{1,0:T(8,128)(2,1)}, bf16[256,256]{1,0:T(8,128)(2,1)S(1)}, u32[]{:S(2)}, u32[]{:S(2)}) %collective-permute-start.19) | collective-permute-done | bytes 131104 | tf_op jit(solution)/shard_map/ppermute | solution.py:469
  104.9 0.6 copy-done.22
  105.5 0.0 copy-done.23
  105.6 0.1 copy-done.24
  105.6 5.3 %finish_rows.1 = f32[1024,256]{1,0:T(8,128)} custom-call(s32[4]{0:T(128)} %compare_select_fusion.1.meta_ref, s32[8,128]{1,0:T(8,128)} %get-tuple-element.30.code_ref, f32[8,128]{1,0:T(8,128)} %bitcast.15, bf16[1024,256]{1,0:T(8,128)(2,1)} %get-tuple-element.46.layer_ref, bf16[256,256]{1,0:T(8,128)(2,1)} %get-tuple-element.47.refs_0_, ...), custom_call_target="tpu_custom_call" | custom-call | flops 1073741824 | bytes 2621440 | tf_op jit(solution)/shard_map/finish_rows/pallas_call | solution.py:377
  (62 shorter events, 0.2 us)
Async XLA Ops:
  3.7 30.1 %collective-permute-start = (bf16[2,256,256]{2,1,0:T(8,128)(2,1)}, bf16[2,256,256]{2,1,0:T(8,128)(2,1)S(1)}, u32[]{:S(2)}, u32[]{:S(2)}) collective-permute-start(bf16[2,256,256]{2,1,0:T(8,128)(2,1)} %get-tuple-element.36.refs_4_), channel_id=1, source_target_pairs={{0,28},{4,0},{8,4},{12,8},{16,12},{20,16},{24,20},{28,24},{1,29},{... | collective-permute-start | bytes 786440 | tf_op jit(solution)/shard_map/ppermute | solution.py:403
  7.1 6.4 %copy-start.6 = (bf16[256,1024]{1,0:T(8,128)(2,1)S(1)}, bf16[256,1024]{1,0:T(8,128)(2,1)}, u32[]{:S(2)}) copy-start(bf16[256,1024]{1,0:T(8,128)(2,1)} %param.11) | copy-start | bytes 1572868
  7.1 9.9 %copy-start.15 = (s32[32,2]{0,1:T(2,128)S(1)}, s32[32,2]{0,1:T(2,128)}, u32[]{:S(2)}) copy-start(s32[32,2]{0,1:T(2,128)} %param.12) | copy-start | bytes 772
  7.1 27.4 %collective-permute-start.1 = (bf16[2,256,256]{2,1,0:T(8,128)(2,1)}, bf16[2,256,256]{2,1,0:T(8,128)(2,1)S(1)}, u32[]{:S(2)}, u32[]{:S(2)}) collective-permute-start(bf16[2,256,256]{2,1,0:T(8,128)(2,1)} %get-tuple-element.39.refs_7_), channel_id=1, source_target_pairs={{0,4},{4,8},{8,12},{12,16},{16,20},{20,24},{24,28},{28,0},{1,5},{5... | collective-permute-start | bytes 786440 | tf_op jit(solution)/shard_map/ppermute | solution.py:403
  10.8 27.7 %collective-permute-start.10 = (bf16[2,256,256]{2,1,0:T(8,128)(2,1)}, bf16[2,256,256]{2,1,0:T(8,128)(2,1)S(1)}, u32[]{:S(2)}, u32[]{:S(2)}) collective-permute-start(bf16[2,256,256]{2,1,0:T(8,128)(2,1)} %get-tuple-element.38.refs_6_), channel_id=1, source_target_pairs={{0,4},{4,8},{8,12},{12,16},{16,20},{20,24},{24,28},{28,0},{1,5},{5... | collective-permute-start | bytes 786440 | tf_op jit(solution)/shard_map/ppermute | solution.py:403
  10.8 27.7 %collective-permute-start.9 = (bf16[2,256,256]{2,1,0:T(8,128)(2,1)}, bf16[2,256,256]{2,1,0:T(8,128)(2,1)S(1)}, u32[]{:S(2)}, u32[]{:S(2)}) collective-permute-start(bf16[2,256,256]{2,1,0:T(8,128)(2,1)} %get-tuple-element.37.refs_5_), channel_id=1, source_target_pairs={{0,28},{4,0},{8,4},{12,8},{16,12},{20,16},{24,20},{28,24},{1,29},{... | collective-permute-start | bytes 786440 | tf_op jit(solution)/shard_map/ppermute | solution.py:403
  13.5 20.3 %copy-start = (bf16[256,512]{1,0:T(8,128)(2,1)}, bf16[256,512]{1,0:T(8,128)(2,1)S(1)}, u32[]{:S(2)}) copy-start(bf16[256,512]{1,0:T(8,128)(2,1)S(1)} %get-tuple-element.56.refs_4_) | copy-start | bytes 786436
  13.5 32.8 %collective-permute-start.5 = (bf16[256,512]{1,0:T(8,128)(2,1)S(1)}, bf16[256,512]{1,0:T(8,128)(2,1)S(1)}, u32[]{:S(2)}, u32[]{:S(2)}) collective-permute-start(bf16[256,512]{1,0:T(8,128)(2,1)S(1)} %get-tuple-element.56.refs_4_), channel_id=1, source_target_pairs={{0,1},{3,2},{4,5},{7,6},{8,9},{11,10},{12,13},{15,14},{16,17},{19,... | collective-permute-start | bytes 786440 | tf_op jit(solution)/shard_map/ppermute | solution.py:406
  33.8 4.8 %copy-start.4 = (bf16[2,256,256]{2,1,0:T(8,128)(2,1)}, bf16[2,256,256]{2,1,0:T(8,128)(2,1)S(1)}, u32[]{:S(2)}) copy-start(bf16[2,256,256]{2,1,0:T(8,128)(2,1)S(1)} %collective-permute-done.refs_6_) | copy-start | bytes 786436
  33.8 19.9 %collective-permute-start.6 = (bf16[256,512]{1,0:T(8,128)(2,1)S(1)}, bf16[256,512]{1,0:T(8,128)(2,1)S(1)}, u32[]{:S(2)}, u32[]{:S(2)}) collective-permute-start(bf16[256,512]{1,0:T(8,128)(2,1)S(1)} %get-tuple-element.55), channel_id=1, source_target_pairs={{1,2},{2,1},{5,6},{6,5},{9,10},{10,9},{13,14},{14,13},{17,18},{18,... | collective-permute-start | bytes 786440 | tf_op jit(solution)/shard_map/ppermute | solution.py:406
  34.5 4.1 %copy-start.5 = (bf16[2,256,256]{2,1,0:T(8,128)(2,1)}, bf16[2,256,256]{2,1,0:T(8,128)(2,1)S(1)}, u32[]{:S(2)}) copy-start(bf16[2,256,256]{2,1,0:T(8,128)(2,1)S(1)} %collective-permute-done.1.refs_7_.refs_8_) | copy-start | bytes 786436
  34.5 20.5 %collective-permute-start.7 = (bf16[256,512]{1,0:T(8,128)(2,1)S(1)}, bf16[256,512]{1,0:T(8,128)(2,1)S(1)}, u32[]{:S(2)}, u32[]{:S(2)}) collective-permute-start(bf16[256,512]{1,0:T(8,128)(2,1)S(1)} %get-tuple-element.55), channel_id=1, source_target_pairs={{0,2},{3,1},{4,6},{7,5},{8,10},{11,9},{12,14},{15,13},{16,18},{19,... | collective-permute-start | bytes 786440 | tf_op jit(solution)/shard_map/ppermute | solution.py:406
  38.5 0.7 copy-start.7
  38.5 0.8 copy-start.8
  44.2 11.5 %collective-permute-start.11 = (bf16[2,256,256]{2,1,0:T(8,128)(2,1)}, bf16[2,256,256]{2,1,0:T(8,128)(2,1)S(1)}, u32[]{:S(2)}, u32[]{:S(2)}) collective-permute-start(bf16[2,256,256]{2,1,0:T(8,128)(2,1)} %finish_attention.3.refs_0_), channel_id=1, source_target_pairs={{0,1},{3,2},{4,5},{7,6},{8,9},{11,10},{12,13},{15,14},{16,17},{19,... | collective-permute-start | bytes 786440 | tf_op jit(solution)/shard_map/ppermute | solution.py:406
  45.6 13.1 %collective-permute-start.12 = (bf16[2,256,256]{2,1,0:T(8,128)(2,1)}, bf16[2,256,256]{2,1,0:T(8,128)(2,1)S(1)}, u32[]{:S(2)}, u32[]{:S(2)}) collective-permute-start(bf16[2,256,256]{2,1,0:T(8,128)(2,1)} %finish_attention.3.refs_0_), channel_id=1, source_target_pairs={{1,2},{2,1},{5,6},{6,5},{9,10},{10,9},{13,14},{14,13},{17,18},{18,... | collective-permute-start | bytes 786440 | tf_op jit(solution)/shard_map/ppermute | solution.py:406
  46.3 12.4 %copy-start.1 = (bf16[256,512]{1,0:T(8,128)(2,1)}, bf16[256,512]{1,0:T(8,128)(2,1)S(1)}, u32[]{:S(2)}) copy-start(bf16[256,512]{1,0:T(8,128)(2,1)S(1)} %collective-permute-done.5.refs_5_) | copy-start | bytes 786436
  46.3 12.4 %collective-permute-start.13 = (bf16[2,256,256]{2,1,0:T(8,128)(2,1)}, bf16[2,256,256]{2,1,0:T(8,128)(2,1)S(1)}, u32[]{:S(2)}, u32[]{:S(2)}) collective-permute-start(bf16[2,256,256]{2,1,0:T(8,128)(2,1)} %finish_attention.3.refs_0_), channel_id=1, source_target_pairs={{0,2},{3,1},{4,6},{7,5},{8,10},{11,9},{12,14},{15,13},{16,18},{19,... | collective-permute-start | bytes 786440 | tf_op jit(solution)/shard_map/ppermute | solution.py:406
  53.7 5.1 %copy-start.2 = (bf16[256,512]{1,0:T(8,128)(2,1)}, bf16[256,512]{1,0:T(8,128)(2,1)S(1)}, u32[]{:S(2)}) copy-start(bf16[256,512]{1,0:T(8,128)(2,1)S(1)} %collective-permute-done.6.refs_6_) | copy-start | bytes 786436
  53.7 11.8 %collective-permute-start.2 = (bf16[2,256,256]{2,1,0:T(8,128)(2,1)}, bf16[2,256,256]{2,1,0:T(8,128)(2,1)S(1)}, u32[]{:S(2)}, u32[]{:S(2)}) collective-permute-start(bf16[2,256,256]{2,1,0:T(8,128)(2,1)} %finish_attention.2.refs_0_), channel_id=1, source_target_pairs={{0,1},{3,2},{4,5},{7,6},{8,9},{11,10},{12,13},{15,14},{16,17},{19,... | collective-permute-start | bytes 786440 | tf_op jit(solution)/shard_map/ppermute | solution.py:406
  55.0 3.7 %copy-start.3 = (bf16[256,512]{1,0:T(8,128)(2,1)}, bf16[256,512]{1,0:T(8,128)(2,1)S(1)}, u32[]{:S(2)}) copy-start(bf16[256,512]{1,0:T(8,128)(2,1)S(1)} %collective-permute-done.7.refs_7_) | copy-start | bytes 786436
  55.0 10.5 %collective-permute-start.3 = (bf16[2,256,256]{2,1,0:T(8,128)(2,1)}, bf16[2,256,256]{2,1,0:T(8,128)(2,1)S(1)}, u32[]{:S(2)}, u32[]{:S(2)}) collective-permute-start(bf16[2,256,256]{2,1,0:T(8,128)(2,1)} %finish_attention.2.refs_0_), channel_id=1, source_target_pairs={{1,2},{2,1},{5,6},{6,5},{9,10},{10,9},{13,14},{14,13},{17,18},{18,... | collective-permute-start | bytes 786440 | tf_op jit(solution)/shard_map/ppermute | solution.py:406
  55.7 3.0 %copy-start.9 = (bf16[2,256,256]{2,1,0:T(8,128)(2,1)}, bf16[2,256,256]{2,1,0:T(8,128)(2,1)S(1)}, u32[]{:S(2)}) copy-start(bf16[2,256,256]{2,1,0:T(8,128)(2,1)S(1)} %collective-permute-done.11.refs_1_) | copy-start | bytes 786436
  55.7 9.8 %collective-permute-start.4 = (bf16[2,256,256]{2,1,0:T(8,128)(2,1)}, bf16[2,256,256]{2,1,0:T(8,128)(2,1)S(1)}, u32[]{:S(2)}, u32[]{:S(2)}) collective-permute-start(bf16[2,256,256]{2,1,0:T(8,128)(2,1)} %finish_attention.2.refs_0_), channel_id=1, source_target_pairs={{0,2},{3,1},{4,6},{7,5},{8,10},{11,9},{12,14},{15,13},{16,18},{19,... | collective-permute-start | bytes 786440 | tf_op jit(solution)/shard_map/ppermute | solution.py:406
  58.7 0.7 copy-start.11
  59.4 0.7 copy-start.12
  64.2 21.0 %collective-permute-start.14 = (bf16[2,256,256]{2,1,0:T(8,128)(2,1)}, bf16[2,256,256]{2,1,0:T(8,128)(2,1)S(1)}, u32[]{:S(2)}, u32[]{:S(2)}) collective-permute-start(bf16[2,256,256]{2,1,0:T(8,128)(2,1)} %get-tuple-element.45), channel_id=1, source_target_pairs={{1,0},{2,3},{5,4},{6,7},{9,8},{10,11},{13,12},{14,15},{17,16},{18,... | collective-permute-start | bytes 786440 | tf_op jit(solution)/shard_map/ppermute | solution.py:406
  65.4 0.7 copy-start.10
  65.5 0.8 copy-start.13
  66.2 0.7 copy-start.14
  71.0 14.2 %collective-permute-start.8 = (bf16[2,256,256]{2,1,0:T(8,128)(2,1)}, bf16[2,256,256]{2,1,0:T(8,128)(2,1)S(1)}, u32[]{:S(2)}, u32[]{:S(2)}) collective-permute-start(bf16[2,256,256]{2,1,0:T(8,128)(2,1)} %get-tuple-element.43), channel_id=1, source_target_pairs={{1,0},{2,3},{5,4},{6,7},{9,8},{10,11},{13,12},{14,15},{17,16},{18,... | collective-permute-start | bytes 786440 | tf_op jit(solution)/shard_map/ppermute | solution.py:406
  85.2 0.7 copy-start.16
  85.2 0.8 copy-start.17
  89.4 3.5 %collective-permute-start.15 = (bf16[256,256]{1,0:T(8,128)(2,1)}, bf16[256,256]{1,0:T(8,128)(2,1)S(1)}, u32[]{:S(2)}, u32[]{:S(2)}) collective-permute-start(bf16[256,256]{1,0:T(8,128)(2,1)} %get-tuple-element.48), channel_id=1, source_target_pairs={{0,4},{4,0},{8,12},{12,8},{16,20},{20,16},{24,28},{28,24},{1,5},{5... | collective-permute-start | bytes 393224 | tf_op jit(solution)/shard_map/ppermute | solution.py:469
  89.4 6.6 %collective-permute-start.16 = (bf16[256,256]{1,0:T(8,128)(2,1)}, bf16[256,256]{1,0:T(8,128)(2,1)S(1)}, u32[]{:S(2)}, u32[]{:S(2)}) collective-permute-start(bf16[256,256]{1,0:T(8,128)(2,1)} %get-tuple-element.49), channel_id=1, source_target_pairs={{0,8},{4,12},{8,0},{12,4},{16,24},{20,28},{24,16},{28,20},{1,9},{5... | collective-permute-start | bytes 393224 | tf_op jit(solution)/shard_map/ppermute | solution.py:469
  90.0 7.8 %collective-permute-start.17 = (bf16[256,256]{1,0:T(8,128)(2,1)}, bf16[256,256]{1,0:T(8,128)(2,1)S(1)}, u32[]{:S(2)}, u32[]{:S(2)}) collective-permute-start(bf16[256,256]{1,0:T(8,128)(2,1)} %get-tuple-element.50), channel_id=1, source_target_pairs={{0,12},{4,8},{8,4},{12,0},{16,28},{20,24},{24,20},{28,16},{1,13},{... | collective-permute-start | bytes 393224 | tf_op jit(solution)/shard_map/ppermute | solution.py:469
  91.2 6.6 %collective-permute-start.18 = (bf16[256,256]{1,0:T(8,128)(2,1)}, bf16[256,256]{1,0:T(8,128)(2,1)S(1)}, u32[]{:S(2)}, u32[]{:S(2)}) collective-permute-start(bf16[256,256]{1,0:T(8,128)(2,1)} %get-tuple-element.51), channel_id=1, source_target_pairs={{0,16},{4,20},{8,24},{12,28},{16,0},{20,4},{24,8},{28,12},{1,17},{... | collective-permute-start | bytes 393224 | tf_op jit(solution)/shard_map/ppermute | solution.py:469
  91.8 13.1 %collective-permute-start.19 = (bf16[256,256]{1,0:T(8,128)(2,1)}, bf16[256,256]{1,0:T(8,128)(2,1)S(1)}, u32[]{:S(2)}, u32[]{:S(2)}) collective-permute-start(bf16[256,256]{1,0:T(8,128)(2,1)} %get-tuple-element.52), channel_id=1, source_target_pairs={{0,20},{4,16},{8,28},{12,24},{16,4},{20,0},{24,12},{28,8},{1,21},{... | collective-permute-start | bytes 393224 | tf_op jit(solution)/shard_map/ppermute | solution.py:469
  92.9 12.0 %copy-start.18 = (bf16[256,256]{1,0:T(8,128)(2,1)}, bf16[256,256]{1,0:T(8,128)(2,1)S(1)}, u32[]{:S(2)}) copy-start(bf16[256,256]{1,0:T(8,128)(2,1)S(1)} %collective-permute-done.15.refs_1_) | copy-start | bytes 393220
  92.9 12.0 %collective-permute-start.20 = (bf16[256,256]{1,0:T(8,128)(2,1)}, bf16[256,256]{1,0:T(8,128)(2,1)S(1)}, u32[]{:S(2)}, u32[]{:S(2)}) collective-permute-start(bf16[256,256]{1,0:T(8,128)(2,1)} %get-tuple-element.53), channel_id=1, source_target_pairs={{0,24},{4,28},{8,16},{12,20},{16,8},{20,12},{24,0},{28,4},{1,25},{... | collective-permute-start | bytes 393224 | tf_op jit(solution)/shard_map/ppermute | solution.py:469
  95.9 8.9 %copy-start.19 = (bf16[256,256]{1,0:T(8,128)(2,1)}, bf16[256,256]{1,0:T(8,128)(2,1)S(1)}, u32[]{:S(2)}) copy-start(bf16[256,256]{1,0:T(8,128)(2,1)S(1)} %collective-permute-done.16.refs_2_) | copy-start | bytes 393220
  95.9 8.9 %collective-permute-start.21 = (bf16[256,256]{1,0:T(8,128)(2,1)}, bf16[256,256]{1,0:T(8,128)(2,1)S(1)}, u32[]{:S(2)}, u32[]{:S(2)}) collective-permute-start(bf16[256,256]{1,0:T(8,128)(2,1)} %get-tuple-element.54), channel_id=1, source_target_pairs={{0,28},{4,24},{8,20},{12,16},{16,12},{20,8},{24,4},{28,0},{1,29},{... | collective-permute-start | bytes 393224 | tf_op jit(solution)/shard_map/ppermute | solution.py:469
  97.8 7.1 %copy-start.20 = (bf16[256,256]{1,0:T(8,128)(2,1)}, bf16[256,256]{1,0:T(8,128)(2,1)S(1)}, u32[]{:S(2)}) copy-start(bf16[256,256]{1,0:T(8,128)(2,1)S(1)} %collective-permute-done.17.refs_3_) | copy-start | bytes 393220
  97.9 7.1 %copy-start.21 = (bf16[256,256]{1,0:T(8,128)(2,1)}, bf16[256,256]{1,0:T(8,128)(2,1)S(1)}, u32[]{:S(2)}) copy-start(bf16[256,256]{1,0:T(8,128)(2,1)S(1)} %collective-permute-done.18.refs_4_) | copy-start | bytes 393220
  104.8 0.7 copy-start.22
  104.9 0.7 copy-start.23
  104.9 0.7 copy-start.24
